TPU v7x, 32 devices: a whole 2x2x4 slice. The times are simulated.
32 devices in a mesh: pix: 16 (over z, x, core), rep: 2 (over y).
Axes of the slice: x: 2, y: 2, z: 4, core: 2. Of those that a mesh axis runs over, the one named last changes fastest.
Arguments:
- tokens: bfloat16 [256, 16, 1152], P(('pix', 'rep')), may hold values from -48 to 48
- out_grad: bfloat16 [256, 16, 1152], P(('pix', 'rep')), may hold values from -6 to 6
- query_weight: bfloat16 [1152, 1152], P('pix'), may hold values from -0.1875 to 0.1875
- key_weight: bfloat16 [1152, 1152], P('pix'), may hold values from -0.1875 to 0.1875
- value_weight: bfloat16 [1152, 1152], P('pix'), may hold values from -0.1875 to 0.1875
- output_weight: bfloat16 [1152, 1152], P('pix'), may hold values from -0.1875 to 0.1875
Outputs:
- input_grad: bfloat16 [256, 16, 1152], P(('pix', 'rep'))
- weight_grads: float32 [1152, 4608], P('pix')
All inputs are finite; a program needn't handle non-finite values.
Results may differ from a plain program's by a relative error of at most 0.025.
The roundings to bfloat16 on the way count: a program that leaves them out, or rounds other values in their place, can miss the bound.
Values may be sent and summed in bfloat16 or wider, within the bound.
No kernel may reach another device: no remote copies, remote signals or barrier semaphores. Data moves between devices by JAX's collectives and lax.ppermute only.
A program may use at most 128 MiB of HBM per device.

v0:
```python
import jax
import jax.numpy as jnp
from jax import lax
from jax.sharding import PartitionSpec as P

D = 1152
HEADS = 16
HEAD_DIM = 72
FRAMES = 16


def contract_last(left, right):
    return lax.dot_general(
        left, right, (((1,), (1,)), ((), ())), preferred_element_type=jnp.float32
    )


def contract_first(left, right):
    return lax.dot_general(
        left, right, (((0,), (0,)), ((), ())), preferred_element_type=jnp.float32
    )


def local(tokens, out_grad, query_weight, key_weight, value_weight, output_weight):
    count = tokens.shape[0]
    rows = tokens.reshape(-1, D)
    drows = out_grad.reshape(-1, D)
    scale = 1.0 / HEAD_DIM**0.5
    full_q, full_k, full_v = (
        lax.all_gather(query_weight, "pix", axis=0, tiled=True),
        lax.all_gather(key_weight, "pix", axis=0, tiled=True),
        lax.all_gather(value_weight, "pix", axis=0, tiled=True),
    )
    query = jnp.dot(rows, full_q, preferred_element_type=jnp.float32).astype(jnp.bfloat16)
    keyed = jnp.dot(rows, full_k, preferred_element_type=jnp.float32).astype(jnp.bfloat16)
    valued = jnp.dot(rows, full_v, preferred_element_type=jnp.float32).astype(jnp.bfloat16)
    shape4 = (count, FRAMES, HEADS, HEAD_DIM)
    qh = query.reshape(shape4)
    kh = keyed.reshape(shape4)
    vh = valued.reshape(shape4)
    scores = jnp.einsum("sfhe,sghe->shfg", qh, kh, preferred_element_type=jnp.float32) * scale
    scores = scores - jnp.max(scores, axis=-1, keepdims=True)
    expo = jnp.exp(scores)
    probs = expo / jnp.sum(expo, axis=-1, keepdims=True)
    probs_b = probs.astype(jnp.bfloat16)
    attended = (
        jnp.einsum("shfg,sghe->sfhe", probs_b, vh, preferred_element_type=jnp.float32)
        .reshape(-1, D)
        .astype(jnp.bfloat16)
    )
    output_full = lax.all_gather(output_weight, "pix", axis=0, tiled=True)
    dattn = contract_last(drows, output_full).astype(jnp.bfloat16)
    dah = dattn.reshape(shape4)
    dvalue = (
        jnp.einsum("shfg,sfhe->sghe", probs_b, dah, preferred_element_type=jnp.float32)
        .reshape(-1, D)
        .astype(jnp.bfloat16)
    )
    dprobs = jnp.einsum("sfhe,sghe->shfg", dah, vh, preferred_element_type=jnp.float32)
    dscore = (probs * (dprobs - jnp.sum(dprobs * probs, axis=-1, keepdims=True)) * scale).astype(
        jnp.bfloat16
    )
    dquery = (
        jnp.einsum("shfg,sghe->sfhe", dscore, kh, preferred_element_type=jnp.float32)
        .reshape(-1, D)
        .astype(jnp.bfloat16)
    )
    dkey = (
        jnp.einsum("shfg,sfhe->sghe", dscore, qh, preferred_element_type=jnp.float32)
        .reshape(-1, D)
        .astype(jnp.bfloat16)
    )
    grads = lax.psum_scatter(
        jnp.concatenate(
            [
                jnp.concatenate(
                    [
                        contract_first(rows, dquery),
                        contract_first(rows, dkey),
                        contract_first(rows, dvalue),
                    ],
                    axis=1,
                ),
                contract_first(attended, drows),
            ],
            axis=1,
        ).astype(jnp.bfloat16),
        "pix",
        scatter_dimension=0,
        tiled=True,
    ).astype(jnp.float32)
    back_q, back_k, back_v = (
        lax.all_gather(query_weight, "pix", axis=0, tiled=True),
        lax.all_gather(key_weight, "pix", axis=0, tiled=True),
        lax.all_gather(value_weight, "pix", axis=0, tiled=True),
    )
    dinput = (
        contract_last(dquery, back_q) + contract_last(dkey, back_k) + contract_last(dvalue, back_v)
    )
    weight_grads = lax.psum(grads, "rep")
    return (dinput.astype(jnp.bfloat16).reshape(tokens.shape), weight_grads)


def solution(mesh):
    placed = (
        P(("pix", "rep"), None, None),
        P(("pix", "rep"), None, None),
        P("pix", None),
        P("pix", None),
        P("pix", None),
        P("pix", None),
    )
    return jax.shard_map(
        local,
        mesh=mesh,
        in_specs=placed,
        out_specs=(P(("pix", "rep"), None, None), P("pix", None)),
        check_vma=False,
    )
```

profile of v0, /device:TPU:0, one launch (start us, length us, event | category | flops | bytes accessed | tf_op | source)
XLA Modules:
  0.0 441.2 jit_solution(11428805849281007432)
XLA Ops:
  10.0 46.1 %all-gather.9.cloned.1.call-done = bf16[1152,1152]{1,0:T(8,128)(2,1)} async-done(((bf16[72,1152]{1,0:T(8,128)(2,1)}), bf16[1152,1152]{1,0:T(8,128)(2,1)}) %all-gather.9.cloned.1.call-update) | async-done | bytes 2654224 | tf_op jit(solution)/shard_map/all_gather | solution.py:51
  56.1 2.8 convolution_convert_fusion.5
  58.9 0.9 reshape.43
  59.8 40.5 %all-gather.11.cloned.1.call-done = bf16[1152,1152]{1,0:T(8,128)(2,1)} async-done(((bf16[72,1152]{1,0:T(8,128)(2,1)}), bf16[1152,1152]{1,0:T(8,128)(2,1)}) %all-gather.11.cloned.1.call-update) | async-done | bytes 2654224 | tf_op jit(solution)/shard_map/all_gather | solution.py:32
  100.3 2.3 convolution_convert_fusion.4
  102.6 0.9 reshape.44
  103.6 40.9 %all-gather.5.cloned.1.call-done = bf16[1152,1152]{1,0:T(8,128)(2,1)} async-done(((bf16[72,1152]{1,0:T(8,128)(2,1)}), bf16[1152,1152]{1,0:T(8,128)(2,1)}) %all-gather.5.cloned.1.call-update) | async-done | bytes 2654224 | tf_op jit(solution)/shard_map/all_gather | solution.py:31
  144.5 2.3 convolution_convert_fusion.7
  146.8 0.9 reshape.40
  147.8 40.8 %all-gather.7.cloned.1.call-done = bf16[1152,1152]{1,0:T(8,128)(2,1)} async-done(((bf16[72,1152]{1,0:T(8,128)(2,1)}), bf16[1152,1152]{1,0:T(8,128)(2,1)}) %all-gather.7.cloned.1.call-update) | async-done | bytes 2654224 | tf_op jit(solution)/shard_map/all_gather | solution.py:30
  188.6 2.3 convolution_convert_fusion.6
  190.9 0.9 reshape.41
  192.3 1.7 fusion.48
  194.0 2.3 fusion.14
  196.3 2.3 fusion.13
  198.6 3.0 fusion.12
  201.6 1.6 fusion.15
  205.9 0.9 fusion.4
  206.8 0.9 fusion.3
  207.7 0.9 fusion.2
  208.8 0.9 convolution_convert_fusion
  209.7 28.0 %pad_maximum_fusion = bf16[1152,4608]{0,1:T(8,128)(2,1)} fusion(bf16[1152,1152]{0,1:T(8,128)(2,1)S(1)} %convolution_convert_fusion, bf16[1152,1152]{0,1:T(8,128)(2,1)S(1)} %fusion.4, bf16[1152,1152]{0,1:T(8,128)(2,1)S(1)} %fusion.3, bf16[1152,1152]{0,1:T(8,128)(2,1)S(1)} %fusion.2), kind=kLoop, calls=%fused_computation.2 | loop fusion | flops 42467328 | bytes 21233664 | tf_op jit(solution)/shard_map/concatenate | solution.py:74
  237.7 15.3 %copy.51 = bf16[1152,4608]{1,0:T(8,128)(2,1)} copy(bf16[1152,4608]{0,1:T(8,128)(2,1)} %pad_maximum_fusion) | data formatting | bytes 21233664
  253.0 1.7 copy-done.2
  254.7 0.9 fusion.53
  256.5 0.9 convolution_add_fusion.1
  257.4 1.2 copy-done.3
  258.7 1.6 fusion.5
  260.3 112.4 %reduce-scatter.4.cloned.1.call-done = bf16[72,4608]{1,0:T(8,128)(2,1)} async-done(((bf16[1152,4608]{1,0:T(8,128)(2,1)}), bf16[72,4608]{1,0:T(8,128)(2,1)}) %reduce-scatter.4.cloned.1.call-update) | async-done | bytes 663568
  372.7 2.3 copy.52
  375.0 57.9 %all-reduce.1 = f32[72,4608]{0,1:T(8,128)S(1)} all-reduce(bf16[72,4608]{0,1:T(8,128)(2,1)} %copy.52), channel_id=1, replica_groups=mesh['pix'=16,'rep'=2] {'rep'}, use_global_device_ids=true, to_apply=%region_4.0 | all-reduce | flops 331776 | bytes 1990656 | tf_op jit(solution)/shard_map/psum | solution.py:100
  432.9 1.7 copy.48
  (37 shorter events, 6.6 us)
Async XLA Ops:
  7.2 93.1 %copy-start = (bf16[8,16,1152]{2,1,0:T(8,128)(2,1)S(1)}, bf16[8,16,1152]{2,1,0:T(8,128)(2,1)}, u32[]{:S(2)}) copy-start(bf16[8,16,1152]{2,1,0:T(8,128)(2,1)} %param.6) | copy-start | bytes 884740
  7.2 48.9 %all-gather.9.cloned.1.call-start = ((), (), s32[]{:S(2)}) async-start(), calls=%async_computation.3 | async-start | bytes 2820096 | tf_op jit(solution)/shard_map/all_gather | solution.py:51
  7.9 92.4 %all-gather.11.cloned.1.call-start = ((), (), s32[]{:S(2)}) async-start(), calls=%async_computation.4 | async-start | bytes 2820096 | tf_op jit(solution)/shard_map/all_gather | solution.py:32
  8.7 135.8 %all-gather.5.cloned.1.call-start = ((), (), s32[]{:S(2)}) async-start(), calls=%async_computation.1 | async-start | bytes 2820096 | tf_op jit(solution)/shard_map/all_gather | solution.py:31
  9.4 179.2 %all-gather.7.cloned.1.call-start = ((), (), s32[]{:S(2)}) async-start(), calls=%async_computation.2 | async-start | bytes 2820096 | tf_op jit(solution)/shard_map/all_gather | solution.py:30
  10.0 362.7 %reduce-scatter.4.cloned.1.call-start = ((), (), s32[]{:S(2)}) async-start(), calls=%async_computation.5 | async-start | bytes 11280384
  191.9 2.1 copy-start.9
  201.6 1.7 copy-start.8
  203.3 1.3 copy-start.7
  203.9 2.0 copy-start.4
  206.8 1.8 copy-start.6
  253.0 1.7 copy-start.2
  254.7 1.7 copy-start.1
  256.5 2.2 copy-start.3
  256.5 2.2 copy-start.5
Sparse Core Ops, SparseCore 0:
  10.1 45.8 all-gather.8
  58.2 42.0 all-gather.10
  102.4 42.0 all-gather.4
  146.5 42.0 all-gather.6
  253.1 119.5 reduce-scatter.3
where the time goes:
time: 442 us; the launch traced here: 441 us
  waiting for transfers between devices  283 us (64%)
  blocking collectives  57.9 us (13%)
  local copies, waits for them, and re-layouts  29.5 us (7%)
  matrix products  28.1 us (6%)
  other arithmetic  28 us (6%)
  between operations  14.2 us (3%)
    unnamed x6, waiting for transfers between devices  115 us
    psum x1, blocking collectives, local(): weight_grads = lax.psum(grads, 'rep')  57.9 us
    all_gather x1, waiting for transfers between devices, local(): output_full = lax.all_gather(output_weight, 'pix', axis=0, tiled=True)  46.1 us
    all_gather x1, waiting for transfers between devices, local(): lax.all_gather(key_weight, 'pix', axis=0, tiled=True)  40.9 us
    all_gather x1, waiting for transfers between devices, local(): lax.all_gather(query_weight, 'pix', axis=0, tiled=True)  40.8 us
    all_gather x1, waiting for transfers between devices, local(): lax.all_gather(value_weight, 'pix', axis=0, tiled=True)  40.5 us
    concatenate x1, other arithmetic, local(): jnp.concatenate([jnp.concatenate([contract_first(rows, dquery), contract_...  28 us
    unnamed x23, local copies, waits for them, and re-layouts  23.2 us
  transfers between devices with their start and end apart: 5, of which 5 were waited for; matrix products, arithmetic and copies ran while one was open for 3% of the time, Pallas kernels for 0%

commit v1 on v0

--- a/solution.py
+++ b/solution.py
@@ -97,7 +97,7 @@
     dinput = (
         contract_last(dquery, back_q) + contract_last(dkey, back_k) + contract_last(dvalue, back_v)
     )
-    weight_grads = lax.psum(grads, "rep")
+    weight_grads = jnp.sum(lax.all_gather(grads, "rep"), axis=0)
     return (dinput.astype(jnp.bfloat16).reshape(tokens.shape), weight_grads)
 
 

time: 442 us -> 425 us (0.962)
  blocking collectives: 57.9 us -> 0 us
  waiting for transfers between devices: 283 us -> 323 us
  local copies, waits for them, and re-layouts: 29.5 us -> 22.5 us
  other arithmetic: 28 us -> 33.3 us
    reduce_scatter x0 -> x1, waiting for transfers between devices: none -> 120 us  [local(): lax.psum_scatter(jnp.concatenate([jnp.concatenate([contract_first(rows, d...]
    unnamed x6, waiting for transfers between devices: 115 us -> 2.61 us
    psum x1 -> x0, blocking collectives: 57.9 us -> none  [local(): weight_grads = lax.psum(grads, 'rep')]
    all_gather x0 -> x1, waiting for transfers between devices: none -> 32.9 us  [local(): weight_grads = jnp.sum(lax.all_gather(grads, 'rep'), axis=0)]
    unnamed x23 -> x19, local copies, waits for them, and re-layouts: 23.2 us -> 16.1 us
  transfers between devices with their start and end apart: 5 -> 6, of which waited for: 5 -> 6; matrix products, arithmetic and copies ran while one was open for 3% -> 4% of each run, Pallas kernels for 0% -> 0%
where the time goes in v1:
time: 425 us; the launch traced here: 424 us
  waiting for transfers between devices  323 us (76%)
  other arithmetic  33.3 us (8%)
  matrix products  30.2 us (7%)
  local copies, waits for them, and re-layouts  22.5 us (5%)
  between operations  14.5 us (3%)
    reduce_scatter x1, waiting for transfers between devices, local(): lax.psum_scatter(jnp.concatenate([jnp.concatenate([contract_first(rows, d...  120 us
    all_gather x1, waiting for transfers between devices, local(): output_full = lax.all_gather(output_weight, 'pix', axis=0, tiled=True)  46.1 us
    all_gather x1, waiting for transfers between devices, local(): lax.all_gather(key_weight, 'pix', axis=0, tiled=True)  40.9 us
    all_gather x1, waiting for transfers between devices, local(): lax.all_gather(query_weight, 'pix', axis=0, tiled=True)  40.8 us
    all_gather x1, waiting for transfers between devices, local(): lax.all_gather(value_weight, 'pix', axis=0, tiled=True)  40.5 us
    all_gather x1, waiting for transfers between devices, local(): weight_grads = jnp.sum(lax.all_gather(grads, 'rep'), axis=0)  32.9 us
    concatenate x1, other arithmetic, local(): jnp.concatenate([jnp.concatenate([contract_first(rows, dquery), contract_...  28 us
    unnamed x19, local copies, waits for them, and re-layouts  16.1 us
  transfers between devices with their start and end apart: 6, of which 6 were waited for; matrix products, arithmetic and copies ran while one was open for 4% of the time, Pallas kernels for 0%

profile of v1, /device:TPU:0, one launch (start us, length us, event | category | flops | bytes accessed | tf_op | source)
XLA Modules:
  0.0 424.2 jit_solution(10470038934049325147)
XLA Ops:
  8.0 0.7 all-gather.13.cloned.1.call-update
  10.0 46.1 %all-gather.11.cloned.1.call-done = bf16[1152,1152]{1,0:T(8,128)(2,1)} async-done(((bf16[72,1152]{1,0:T(8,128)(2,1)}), bf16[1152,1152]{1,0:T(8,128)(2,1)}) %all-gather.11.cloned.1.call-update) | async-done | bytes 2654224 | tf_op jit(solution)/shard_map/all_gather | solution.py:51
  56.1 2.8 convolution_convert_fusion.5
  58.9 0.9 reshape.43
  59.8 40.5 %all-gather.13.cloned.1.call-done = bf16[1152,1152]{1,0:T(8,128)(2,1)} async-done(((bf16[72,1152]{1,0:T(8,128)(2,1)}), bf16[1152,1152]{1,0:T(8,128)(2,1)}) %all-gather.13.cloned.1.call-update) | async-done | bytes 2654224 | tf_op jit(solution)/shard_map/all_gather | solution.py:32
  100.3 2.3 convolution_convert_fusion.4
  102.6 0.9 reshape.44
  103.6 40.9 %all-gather.7.cloned.1.call-done = bf16[1152,1152]{1,0:T(8,128)(2,1)} async-done(((bf16[72,1152]{1,0:T(8,128)(2,1)}), bf16[1152,1152]{1,0:T(8,128)(2,1)}) %all-gather.7.cloned.1.call-update) | async-done | bytes 2654224 | tf_op jit(solution)/shard_map/all_gather | solution.py:31
  144.5 2.3 convolution_convert_fusion.7
  146.8 0.9 reshape.40
  147.8 40.8 %all-gather.9.cloned.1.call-done = bf16[1152,1152]{1,0:T(8,128)(2,1)} async-done(((bf16[72,1152]{1,0:T(8,128)(2,1)}), bf16[1152,1152]{1,0:T(8,128)(2,1)}) %all-gather.9.cloned.1.call-update) | async-done | bytes 2654224 | tf_op jit(solution)/shard_map/all_gather | solution.py:30
  188.6 2.3 convolution_convert_fusion.6
  190.9 0.9 reshape.41
  192.3 1.7 fusion.48
  194.0 2.3 fusion.14
  196.3 2.3 fusion.13
  198.6 3.2 fusion.12
  201.7 1.6 fusion.15
  206.0 0.9 fusion.4
  206.9 0.9 fusion.3
  207.8 0.9 fusion.2
  208.9 0.9 convolution_convert_fusion
  209.8 28.0 %pad_maximum_fusion = bf16[1152,4608]{0,1:T(8,128)(2,1)} fusion(bf16[1152,1152]{0,1:T(8,128)(2,1)S(1)} %convolution_convert_fusion, bf16[1152,1152]{0,1:T(8,128)(2,1)S(1)} %fusion.4, bf16[1152,1152]{0,1:T(8,128)(2,1)S(1)} %fusion.3, bf16[1152,1152]{0,1:T(8,128)(2,1)S(1)} %fusion.2), kind=kLoop, calls=%fused_computation.2 | loop fusion | flops 42467328 | bytes 21233664 | tf_op jit(solution)/shard_map/concatenate | solution.py:74
  237.8 15.3 %copy.65 = bf16[1152,4608]{1,0:T(8,128)(2,1)} copy(bf16[1152,4608]{0,1:T(8,128)(2,1)} %pad_maximum_fusion) | data formatting | bytes 21233664
  253.1 119.6 %reduce-scatter.4.cloned.1.call-done = bf16[72,4608]{1,0:T(8,128)(2,1)} async-done(((bf16[1152,4608]{1,0:T(8,128)(2,1)}), bf16[72,4608]{1,0:T(8,128)(2,1)}) %reduce-scatter.4.cloned.1.call-update) | async-done | bytes 663568 | tf_op jit(solution)/shard_map/reduce_scatter | solution.py:73
  372.7 2.3 all_gather.31
  375.0 2.8 fusion.53
  377.9 0.9 convolution_add_fusion.1
  378.8 0.8 copy-done.2
  379.6 1.6 fusion.5
  381.2 32.9 %all-gather.15.cloned.1.call-done = f32[144,4608]{1,0:T(8,128)} async-done(((f32[72,4608]{1,0:T(8,128)}), f32[144,4608]{1,0:T(8,128)}) %all-gather.15.cloned.1.call-update) | async-done | bytes 2654224 | tf_op jit(solution)/shard_map/all_gather | solution.py:100
  414.2 3.1 reduce_sum.29
  (37 shorter events, 5.2 us)
Async XLA Ops:
  7.2 93.1 %copy-start = (bf16[8,16,1152]{2,1,0:T(8,128)(2,1)S(1)}, bf16[8,16,1152]{2,1,0:T(8,128)(2,1)}, u32[]{:S(2)}) copy-start(bf16[8,16,1152]{2,1,0:T(8,128)(2,1)} %param.6) | copy-start | bytes 884740
  7.2 48.9 %all-gather.11.cloned.1.call-start = ((), (), s32[]{:S(2)}) async-start(), calls=%async_computation.3 | async-start | bytes 2820096 | tf_op jit(solution)/shard_map/all_gather | solution.py:51
  7.9 92.4 %all-gather.13.cloned.1.call-start = ((), (), s32[]{:S(2)}) async-start(), calls=%async_computation.4 | async-start | bytes 2820096 | tf_op jit(solution)/shard_map/all_gather | solution.py:32
  8.7 135.8 %all-gather.7.cloned.1.call-start = ((), (), s32[]{:S(2)}) async-start(), calls=%async_computation.1 | async-start | bytes 2820096 | tf_op jit(solution)/shard_map/all_gather | solution.py:31
  9.4 179.2 %all-gather.9.cloned.1.call-start = ((), (), s32[]{:S(2)}) async-start(), calls=%async_computation.2 | async-start | bytes 2820096 | tf_op jit(solution)/shard_map/all_gather | solution.py:30
  10.0 362.8 %reduce-scatter.4.cloned.1.call-start = ((), (), s32[]{:S(2)}) async-start(), calls=%async_computation.6 | async-start | bytes 11280384 | tf_op jit(solution)/shard_map/reduce_scatter | solution.py:73
  191.9 2.1 copy-start.8
  201.7 1.6 copy-start.7
  203.4 1.3 copy-start.6
  204.1 2.0 copy-start.3
  206.9 1.8 copy-start.5
  253.1 161.1 %all-gather.15.cloned.1.call-start = ((), (), s32[]{:S(2)}) async-start(), calls=%async_computation.5 | async-start | bytes 3981312 | tf_op jit(solution)/shard_map/all_gather | solution.py:100
  375.0 2.8 copy-start.1
  377.9 1.8 copy-start.2
  377.9 1.8 copy-start.4
Sparse Core Ops, SparseCore 0:
  10.1 45.8 all-gather.10
  58.2 42.0 all-gather.12
  102.4 42.0 all-gather.6
  146.5 42.0 all-gather.8
  253.2 119.5 reduce-scatter.3
  375.1 38.9 all-gather.14
